TPU v7x, 32 devices: a whole 2x2x4 slice. The times are simulated.
32 devices in a mesh: dp: 16 (over z, y, x), ctx: 2 (over core).
Axes of the slice: x: 2, y: 2, z: 4, core: 2. Of those that a mesh axis runs over, the one named last changes fastest.
Arguments:
- inputs: bfloat16 [16, 4, 16, 16, 128], P('dp', 'ctx'), may hold values from -90 to 90
- cotangent: bfloat16 [16, 4, 16, 16, 128], P('dp', 'ctx'), may hold values from -18 to 18
- conv_weight: bfloat16 [3, 3, 3, 128, 128], replicated, may hold values from -0.109375 to 0.109375
- norm_gain: float32 [128], replicated, may hold values from 0.1 to 1.9
- norm_bias: float32 [128], replicated, may hold values from -3 to 3
Outputs:
- input_grad: bfloat16 [16, 4, 16, 16, 128], P('dp', 'ctx')
- weight_grad: float32 [3, 3, 3, 128, 128], replicated
- gain_grad: float32 [128], replicated
- bias_grad: float32 [128], replicated
All inputs are finite; a program needn't handle non-finite values.
Results may differ from a plain program's by a relative error of at most 0.0027.
Values may be sent and summed in bfloat16 or wider, within the bound.
A program may use at most 64 MiB of HBM per device.

v0:
```python
import jax
import jax.numpy as jnp
from jax import lax
from jax.sharding import PartitionSpec as P

GROUPS = 32


epsilon = 1e-06


def from_behind(x, axis, by):
    count = lax.axis_size(axis)
    pairs = [(i, i + by) for i in range(count) if 0 <= i + by < count]
    return lax.ppermute(x, axis, pairs)


def group_average(per_channel, members):
    grouped = per_channel.reshape(GROUPS, -1).sum(axis=1, keepdims=True) / members
    return jnp.broadcast_to(grouped, (GROUPS, per_channel.shape[0] // GROUPS)).reshape(-1)


def kernel_terms(padded_act, grad_flat, frames_n, side_len, channels):
    pieces = []
    for tap_time in range(3):
        for tap_row in range(3):
            columns = jnp.concatenate(
                [
                    padded_act[
                        tap_time : tap_time + frames_n,
                        tap_row : tap_row + side_len,
                        tap_col : tap_col + side_len,
                    ]
                    for tap_col in range(3)
                ],
                axis=-1,
            ).reshape(-1, 3 * channels)
            pieces.append(
                lax.dot_general(
                    columns, grad_flat, (((0,), (0,)), ((), ())), preferred_element_type=jnp.float32
                )
            )
    return jnp.stack(pieces).reshape(3, 3, 3, channels, channels)


def spread_back(grad_ext, weight_turned, frames_out, side_len, channels):
    total_grad = jnp.zeros((frames_out * side_len * side_len, channels), jnp.float32)
    for tap_time in range(3):
        for tap_row in range(3):
            columns = jnp.concatenate(
                [
                    grad_ext[
                        2 - tap_time : 2 - tap_time + frames_out,
                        2 - tap_row : 2 - tap_row + side_len,
                        2 - tap_col : 2 - tap_col + side_len,
                    ]
                    for tap_col in range(3)
                ],
                axis=-1,
            ).reshape(-1, 3 * channels)
            total_grad = total_grad + jnp.dot(
                columns,
                weight_turned[tap_time, tap_row].reshape(3 * channels, channels),
                preferred_element_type=jnp.float32,
            )
    return total_grad.reshape(frames_out, side_len, side_len, channels)


def plane_back(plane, weight_plane, side_len, channels):
    padded = jnp.pad(plane, ((1, 1), (1, 1), (0, 0)))
    total_grad = jnp.zeros((side_len * side_len, channels), jnp.float32)
    for tap_row in range(3):
        columns = jnp.concatenate(
            [
                padded[2 - tap_row : 2 - tap_row + side_len, 2 - tap_col : 2 - tap_col + side_len]
                for tap_col in range(3)
            ],
            axis=-1,
        ).reshape(-1, 3 * channels)
        total_grad = total_grad + jnp.dot(
            columns,
            weight_plane[tap_row].reshape(3 * channels, channels),
            preferred_element_type=jnp.float32,
        )
    return total_grad.reshape(side_len, side_len, channels)


def body(inputs, cotangent, conv_weight, norm_gain, norm_bias):
    frames_n, side_len, channels = (inputs.shape[1], inputs.shape[2], inputs.shape[4])
    ctx_count = lax.axis_size("ctx")
    leading = lax.axis_index("ctx") == 0
    members = frames_n * side_len * side_len * ctx_count * (channels // GROUPS)
    values = inputs[0].astype(jnp.float32)
    flat_values = values.reshape(-1, channels)
    totals, squares = lax.psum(
        (flat_values.sum(axis=0), (flat_values * flat_values).sum(axis=0)), "ctx"
    )
    average = group_average(totals, members)
    spread = group_average(squares, members) - average * average
    inverse_std = lax.rsqrt(spread + epsilon)
    normed_val = (values - average) * inverse_std
    shifted_val = normed_val * norm_gain + norm_bias
    activation = jax.nn.silu(shifted_val).astype(jnp.bfloat16)
    prior = from_behind(activation, "ctx", 1)
    prior = jnp.where(leading, jnp.broadcast_to(activation[:1], prior.shape), prior)
    padded_act = jnp.concatenate([prior, activation], axis=0)
    padded_act = jnp.pad(padded_act, ((0, 0), (1, 1), (1, 1), (0, 0)))
    grad_local = cotangent[0]
    after_frames = from_behind(grad_local, "ctx", -1)
    kernel_sum = kernel_terms(
        padded_act, grad_local.reshape(-1, channels), frames_n, side_len, channels
    )
    grad_ext = jnp.concatenate([grad_local, after_frames], axis=0)
    grad_ext = jnp.pad(grad_ext, ((0, 0), (1, 1), (1, 1), (0, 0)))
    weight_turned = jnp.transpose(conv_weight, (0, 1, 2, 4, 3))
    pad_grad = spread_back(grad_ext, weight_turned, frames_n, side_len, channels)

    def fold_terms():
        first_part = plane_back(grad_local[0], weight_turned[0], side_len, channels)
        second_part = plane_back(grad_local[1], weight_turned[0], side_len, channels)
        third_part = plane_back(grad_local[0], weight_turned[1], side_len, channels)
        return first_part + (second_part + third_part)

    def fold_empty():
        return jnp.zeros((side_len, side_len, channels), jnp.float32)

    folded = lax.cond(leading, fold_terms, fold_empty)
    act_grad = pad_grad.at[0].add(folded)
    sigmoid_val = jax.nn.sigmoid(shifted_val)
    pre_grad = act_grad * sigmoid_val * (1.0 + shifted_val * (1.0 - sigmoid_val))
    normed_grad = pre_grad * norm_gain
    first_total, second_total = lax.psum(
        (
            normed_grad.reshape(-1, channels).sum(axis=0),
            (normed_grad * normed_val).reshape(-1, channels).sum(axis=0),
        ),
        "ctx",
    )
    first_mean = group_average(first_total, members)
    second_mean = group_average(second_total, members)
    input_grad = (inverse_std * (normed_grad - first_mean - normed_val * second_mean)).astype(
        jnp.bfloat16
    )[None]
    gain_part = (pre_grad * normed_val).reshape(-1, channels).sum(axis=0)
    bias_part = pre_grad.reshape(-1, channels).sum(axis=0)
    kernel_all, gain_all, bias_all = lax.psum((kernel_sum, gain_part, bias_part), ("dp", "ctx"))
    cell_total = lax.axis_size("dp") * ctx_count * frames_n * side_len * side_len
    scale_val = 1.0 / jnp.sqrt(jnp.float32(cell_total))
    return (input_grad, kernel_all * scale_val, gain_all * scale_val, bias_all * scale_val)


def solution(mesh):
    placed = (P("dp", "ctx", None, None, None), P("dp", "ctx", None, None, None), P(), P(), P())
    return jax.shard_map(
        body,
        mesh=mesh,
        in_specs=placed,
        out_specs=(P("dp", "ctx", None, None, None), P(), P(), P()),
        check_vma=False,
    )
```

profile of v0, /device:TPU:0, one launch (start us, length us, event | category | flops | bytes accessed | tf_op | source)
XLA Modules:
  0.0 180.4 jit_solution(15650351091484848257)
XLA Ops:
  7.2 1.3 collective-permute-start
  8.5 2.0 %copy.10 = bf16[3,3,3,128,128]{3,4,2,1,0:T(8,128)(2,1)S(1)} copy(bf16[3,3,3,128,128]{4,3,2,1,0:T(8,128)(2,1)} %param.11) | data formatting | bytes 1769472 | tf_op args[2]
  10.6 0.1 fusion.53
  10.8 0.1 reshape.231
  10.9 0.1 reshape.233
  11.0 4.4 %all-reduce.6 = (f32[32,4]{1,0:T(8,128)S(1)}, f32[32,4]{1,0:T(8,128)S(1)}) all-reduce(f32[32,4]{1,0:T(8,128)S(1)} %reshape.233, f32[32,4]{1,0:T(8,128)S(1)} %reshape.231), channel_id=1, replica_groups=mesh['dp'=16,'ctx'=2] {'ctx'}, use_global_device_ids=true, to_apply=%region_4.0 | all-reduce | flops 256 | bytes 2048 | tf_op jit(solution)/shard_map/psum | solution.py:95
  15.4 0.1 reduce_sum.93
  15.5 0.1 reduce_sum.91
  15.7 0.1 reshape.232
  15.9 0.1 reshape.234
  16.0 2.3 %conditional.1 = (f32[1,16,16,128]{3,2,1,0:T(8,128)S(1)}) conditional(s32[]{:T(128)} %convert_element_type.28, () %tuple.20, (bf16[2,16,16,128]{3,2,1,0:T(8,128)(2,1)S(1)}, bf16[3,3,3,128,128]{4,3,2,1,0:T(8,128)(2,1)S(1)}) %tuple.120), branch_computations={%region_6.7_spmd, %region_7.8_spmd} | conditional | flops 230883328 | bytes 9207816 | solution.py:127
  16.1 0.2 pad_slice_fusion.2
  16.3 0.2 fusion.55
  16.5 0.2 convolution_add_fusion.3
  16.7 0.2 convolution_add_fusion.2
  17.0 0.2 fusion.56
  17.2 0.2 fusion.54
  17.4 0.2 convolution_add_fusion.5
  17.6 0.2 convolution_add_fusion.1
  17.8 0.2 convolution_add_fusion.4
  18.0 0.2 fusion.1
  18.3 0.1 pad_slice_fusion.41
  18.5 0.4 pad_slice_fusion.42
  18.9 0.1 pad_maximum_fusion.7
  19.0 0.3 fusion.57
  19.3 0.3 convolution_add_fusion.13
  19.5 0.1 pad_maximum_fusion.9
  19.7 0.3 convolution_add_fusion.12
  19.9 0.3 convolution_add_fusion.11
  20.2 0.1 pad_maximum_fusion.11
  20.3 0.3 convolution_add_fusion.10
  20.6 0.3 convolution_add_fusion.9
  20.9 0.1 pad_maximum_fusion.13
  21.0 0.3 convolution_add_fusion.8
  21.3 0.3 convolution_add_fusion.7
  21.6 0.3 convolution_add_fusion.6
  21.9 0.2 fusion.45
  22.1 0.1 reshape.246
  22.2 0.1 reshape.245
  22.3 3.4 %all-reduce.5 = (f32[32,4]{1,0:T(8,128)S(1)}, f32[32,4]{1,0:T(8,128)S(1)}) all-reduce(f32[32,4]{1,0:T(8,128)S(1)} %reshape.246, f32[32,4]{1,0:T(8,128)S(1)} %reshape.245), channel_id=1, replica_groups=mesh['dp'=16,'ctx'=2] {'ctx'}, use_global_device_ids=true, to_apply=%region_12.13 | all-reduce | flops 256 | bytes 2048 | tf_op jit(solution)/shard_map/psum | solution.py:132
  25.7 0.1 reduce_sum.97
  25.9 0.1 reduce_sum.95
  26.0 0.1 mul.91
  26.2 2.3 %collective-permute-start.1 = (bf16[2,16,16,128]{3,2,1,0:T(8,128)(2,1)S(1)}, bf16[2,16,16,128]{3,2,1,0:T(8,128)(2,1)S(1)}, u32[]{:S(2)}, u32[]{:S(2)}) collective-permute-start(bf16[2,16,16,128]{3,2,1,0:T(8,128)(2,1)S(1)} %get-tuple-element.130), channel_id=1, source_target_pairs={{0,1},{2,3},{4,5},{6,7},{8,9},{10,11},{12,13},{14,15},{16,17},{18,... | collective-permute-start | bytes 393224 | tf_op jit(solution)/shard_map/ppermute | solution.py:15
  28.4 0.9 collective-permute-done.1
  29.5 0.1 pad_slice_fusion.17
  29.6 0.4 pad_slice_fusion.18
  30.1 0.3 fusion.18
  30.5 0.3 fusion.17
  30.9 0.3 fusion.16
  31.3 0.3 fusion.15
  31.7 0.3 fusion.14
  32.0 0.3 fusion.13
  32.4 0.3 fusion.12
  32.8 0.3 fusion.11
  33.1 0.3 fusion.10
  33.5 1.2 copy-done.1
  34.8 0.1 sub.35
  34.9 42.1 %all-reduce.4 = (f32[128]{0:T(128)S(1)}, f32[128]{0:T(128)S(1)}) all-reduce(f32[128]{0:T(128)S(1)} %get-tuple-element.26, f32[128]{0:T(128)S(1)} %get-tuple-element.29), channel_id=1, replica_groups=mesh['dp'=16,'ctx'=2] {'dp','ctx'}, use_global_device_ids=true, to_apply=%region_16.17 | all-reduce | flops 256 | bytes 2048 | tf_op jit(solution)/shard_map/psum | solution.py:146
  77.0 0.5 broadcast_multiply_fusion.2
  77.5 0.5 broadcast_multiply_fusion.1
  78.0 0.7 fusion.46
  78.8 91.9 %all-reduce.9.cloned.1.call-done = f32[3,3,3,128,128]{4,3,2,1,0:T(8,128)} async-done(((f32[3,3,3,128,128]{4,3,2,1,0:T(8,128)}), f32[3,3,3,128,128]{4,3,2,1,0:T(8,128)}) %all-reduce.9.cloned.1.call-update) | async-done | bytes 1769488 | tf_op jit(solution)/shard_map/psum | solution.py:146
  170.7 2.9 %broadcast_multiply_fusion = f32[3,3,3,128,128]{4,3,2,1,0:T(8,128)} fusion(f32[3,3,3,128,128]{4,3,2,1,0:T(8,128)} %all-reduce.9.cloned.1.call-done), kind=kLoop, calls=%fused_computation.113 | loop fusion | flops 442368 | bytes 3538944 | tf_op jit(solution)/shard_map/mul | solution.py:149
  (45 shorter events, 1.3 us)
Async XLA Ops:
  7.2 163.5 %all-reduce.9.cloned.1.call-start = ((), (), s32[]{:S(2)}) async-start(), calls=%async_computation | async-start | bytes 3538944 | tf_op jit(solution)/shard_map/psum | solution.py:146
  7.2 11.1 %collective-permute-start = (bf16[2,16,16,128]{3,2,1,0:T(8,128)(2,1)}, bf16[2,16,16,128]{3,2,1,0:T(8,128)(2,1)S(1)}, u32[]{:S(2)}, u32[]{:S(2)}) collective-permute-start(bf16[2,16,16,128]{3,2,1,0:T(8,128)(2,1)} %bitcast.196), channel_id=1, source_target_pairs={{1,0},{3,2},{5,4},{7,6},{9,8},{11,10},{13,12},{15,14},{17,16},{19,... | collective-permute-start | bytes 393224 | tf_op jit(solution)/shard_map/ppermute | solution.py:15
  8.5 2.2 %copy-start.2 = (bf16[1,2,16,16,128]{4,3,2,1,0:T(8,128)(2,1)S(1)}, bf16[1,2,16,16,128]{4,3,2,1,0:T(8,128)(2,1)}, u32[]{:S(2)}) copy-start(bf16[1,2,16,16,128]{4,3,2,1,0:T(8,128)(2,1)} %param.9) | copy-start | bytes 393220
  8.5 7.3 %copy-start = (bf16[1,2,16,16,128]{4,3,2,1,0:T(8,128)(2,1)S(1)}, bf16[1,2,16,16,128]{4,3,2,1,0:T(8,128)(2,1)}, u32[]{:S(2)}) copy-start(bf16[1,2,16,16,128]{4,3,2,1,0:T(8,128)(2,1)} %param.10) | copy-start | bytes 393220
  21.0 0.9 copy-start.3
  21.0 0.9 copy-start.4
  26.2 3.2 %collective-permute-start.1 = (bf16[2,16,16,128]{3,2,1,0:T(8,128)(2,1)S(1)}, bf16[2,16,16,128]{3,2,1,0:T(8,128)(2,1)S(1)}, u32[]{:S(2)}, u32[]{:S(2)}) collective-permute-start(bf16[2,16,16,128]{3,2,1,0:T(8,128)(2,1)S(1)} %get-tuple-element.130), channel_id=1, source_target_pairs={{0,1},{2,3},{4,5},{6,7},{8,9},{10,11},{12,13},{14,15},{16,17},{18,... | collective-permute-start | bytes 393224 | tf_op jit(solution)/shard_map/ppermute | solution.py:15
  33.5 1.2 copy-start.1
Sparse Core Ops, SparseCore 0:
  34.8 135.8 all-reduce.8
where the time goes:
time: 181 us; the launch traced here: 180 us
  waiting for transfers between devices  92.9 us (51%)
  blocking collectives  49.9 us (28%)
  between operations  14.6 us (8%)
  matrix products  6.96 us (4%)
  other arithmetic  6.58 us (4%)
  local copies, waits for them, and re-layouts  5.8 us (3%)
  starting transfers between devices  3.58 us (2%)
    psum x1, waiting for transfers between devices, body(): lax.psum((kernel_sum, gain_part, bias_part), ('dp', 'ctx'))  91.9 us
    psum x1, blocking collectives, body(): lax.psum((kernel_sum, gain_part, bias_part), ('dp', 'ctx'))  42.1 us
    psum x1, blocking collectives, body(): lax.psum((flat_values.sum(axis=0), (flat_values * flat_values).sum(axis=0...  4.37 us
  transfers between devices with their start and end apart: 3, of which 2 were waited for; matrix products, arithmetic and copies ran while one was open for 4% of the time, Pallas kernels for 0%

commit v1 on v0

--- a/solution.py
+++ b/solution.py
@@ -1,6 +1,9 @@
+import functools
 import jax
 import jax.numpy as jnp
 from jax import lax
+from jax.experimental import pallas as pl
+from jax.experimental.pallas import tpu as pltpu
 from jax.sharding import PartitionSpec as P
 
 GROUPS = 32
@@ -40,7 +43,7 @@
                     columns, grad_flat, (((0,), (0,)), ((), ())), preferred_element_type=jnp.float32
                 )
             )
-    return jnp.stack(pieces).reshape(3, 3, 3, channels, channels)
+    return pieces
 
 
 def spread_back(grad_ext, weight_turned, frames_out, side_len, channels):
@@ -85,6 +88,125 @@
     return total_grad.reshape(side_len, side_len, channels)
 
 
+def step_list(dp_count, ctx_count):
+    steps = []
+    for axis, count in (("ctx", ctx_count), ("dp", dp_count)):
+        bit = 1
+        while bit < count:
+            steps.append((axis, bit))
+            bit *= 2
+    return steps
+
+
+def narrow(step):
+    return step in (1, 2)
+
+
+def sum_kernel(steps, rows, kern_ref, small_ref, out_ref, small_out, acc, gath, *rest):
+    count = len(steps)
+    recvs = rest[:count]
+    sends = dict(zip([i for i in range(count) if narrow(i)], rest[count:]))
+    small_send, small_recv, sems_s, sems_r, small_s, small_r, back_s, back_r = rest[-8:]
+    partners = [{axis: lax.axis_index(axis) ^ bit} for axis, bit in steps]
+    barrier = pltpu.get_barrier_semaphore()
+    for partner in partners:
+        pl.semaphore_signal(
+            barrier, inc=1, device_id=partner, device_id_type=pl.DeviceIdType.MESH
+        )
+    pl.semaphore_wait(barrier, count)
+
+    def remote(src, dst, send_sem, recv_sem, partner):
+        return pltpu.make_async_remote_copy(
+            src_ref=src,
+            dst_ref=dst,
+            send_sem=send_sem,
+            recv_sem=recv_sem,
+            device_id=partner,
+            device_id_type=pl.DeviceIdType.MESH,
+        )
+
+    start = jnp.int32(0)
+    length = rows
+    small_now = small_ref[...]
+    starts = []
+    for i, (axis, bit) in enumerate(steps):
+        starts.append((start, length))
+        half = length // 2
+        mine = (lax.axis_index(axis) // bit) % 2
+        keep = pl.multiple_of(start + mine * half, 16)
+        away = pl.multiple_of(start + (1 - mine) * half, 16)
+        held = kern_ref if i == 0 else acc
+        if narrow(i):
+            sends[i][...] = held[pl.ds(away, half), :].astype(jnp.bfloat16)
+            source = sends[i]
+        else:
+            source = held.at[pl.ds(away, half), :]
+        small_send[i] = small_now
+        copy = remote(source, recvs[i], sems_s.at[i], sems_r.at[i], partners[i])
+        copy.start()
+        small_copy = remote(
+            small_send.at[i], small_recv.at[i], small_s.at[i], small_r.at[i], partners[i]
+        )
+        small_copy.start()
+        copy.wait()
+        acc[pl.ds(keep, half), :] = held[pl.ds(keep, half), :] + recvs[i][...].astype(jnp.float32)
+        small_copy.wait()
+        small_now = small_now + small_recv[i]
+        start = keep
+        length = half
+    small_out[...] = small_now
+    gath[pl.ds(start, length), :] = acc[pl.ds(start, length), :].astype(jnp.bfloat16)
+    for i in reversed(range(count)):
+        piece = gath.at[pl.ds(start, length), :]
+        copy = remote(piece, piece, back_s.at[i], back_r.at[i], partners[i])
+        copy.start()
+        copy.wait()
+        start, length = starts[i]
+        start = pl.multiple_of(start, 16)
+    out_ref[...] = gath[...]
+
+
+def sum_everywhere(pieces, small, channels):
+    steps = step_list(lax.axis_size("dp"), lax.axis_size("ctx"))
+    count = len(steps)
+    devices = 2**count
+    used = sum(piece.shape[0] for piece in pieces)
+    unit = 16 * devices
+    rows = -(-used // unit) * unit
+    blank = jnp.zeros((rows - used, channels), jnp.float32)
+    stacked = jnp.concatenate(list(pieces) + [blank], axis=0)
+    recvs = [
+        pltpu.VMEM((rows >> (i + 1), channels), jnp.bfloat16 if narrow(i) else jnp.float32)
+        for i in range(count)
+    ]
+    sends = [
+        pltpu.VMEM((rows >> (i + 1), channels), jnp.bfloat16) for i in range(count) if narrow(i)
+    ]
+    vmem = pl.BlockSpec(memory_space=pltpu.VMEM)
+    total, small_total = pl.pallas_call(
+        functools.partial(sum_kernel, steps, rows),
+        out_shape=(
+            jax.ShapeDtypeStruct((rows, channels), jnp.bfloat16),
+            jax.ShapeDtypeStruct(small.shape, jnp.float32),
+        ),
+        in_specs=[vmem, vmem],
+        out_specs=(vmem, vmem),
+        scratch_shapes=[
+            pltpu.VMEM((rows, channels), jnp.float32),
+            pltpu.VMEM((rows, channels), jnp.bfloat16),
+            *recvs,
+            *sends,
+            pltpu.VMEM((count,) + small.shape, jnp.float32),
+            pltpu.VMEM((count,) + small.shape, jnp.float32),
+            *[pltpu.SemaphoreType.DMA((count,)) for _ in range(6)],
+        ],
+        compiler_params=pltpu.CompilerParams(
+            collective_id=0, has_side_effects=True, vmem_limit_bytes=48 * 1024 * 1024
+        ),
+    )(stacked, small)
+    return total[:used], small_total
+
+
 def body(inputs, cotangent, conv_weight, norm_gain, norm_bias):
     frames_n, side_len, channels = (inputs.shape[1], inputs.shape[2], inputs.shape[4])
     ctx_count = lax.axis_size("ctx")
@@ -143,7 +265,12 @@
     )[None]
     gain_part = (pre_grad * normed_val).reshape(-1, channels).sum(axis=0)
     bias_part = pre_grad.reshape(-1, channels).sum(axis=0)
-    kernel_all, gain_all, bias_all = lax.psum((kernel_sum, gain_part, bias_part), ("dp", "ctx"))
+    small = jnp.concatenate(
+        [gain_part[None], bias_part[None], jnp.zeros((6, channels), jnp.float32)], axis=0
+    )
+    kernel_all, small_all = sum_everywhere(kernel_sum, small, channels)
+    kernel_all = kernel_all.astype(jnp.float32).reshape(3, 3, 3, channels, channels)
+    gain_all, bias_all = small_all[0], small_all[1]
     cell_total = lax.axis_size("dp") * ctx_count * frames_n * side_len * side_len
     scale_val = 1.0 / jnp.sqrt(jnp.float32(cell_total))
     return (input_grad, kernel_all * scale_val, gain_all * scale_val, bias_all * scale_val)

time: 181 us -> 70.6 us (0.39)
  waiting for transfers between devices: 92.9 us -> 0.01 us
  Pallas kernels: 0 us -> 42.3 us
  blocking collectives: 49.9 us -> 7.77 us
  between operations: 14.6 us -> 1.18 us
  other arithmetic: 6.58 us -> 4.61 us
    psum x1 -> x0, waiting for transfers between devices: 91.9 us -> none  [body(): lax.psum((kernel_sum, gain_part, bias_part), ('dp', 'ctx'))]
    pallas_call x0 -> x1, Pallas kernels: none -> 42.3 us  [sum_everywhere(): pl.pallas_call(functools.partial(sum_kernel, steps, rows), out_shape=(jax...]
    psum x1 -> x0, blocking collectives: 42.1 us -> none  [body(): lax.psum((kernel_sum, gain_part, bias_part), ('dp', 'ctx'))]
  transfers between devices with their start and end apart: 3 -> 2, of which waited for: 2 -> 0; matrix products, arithmetic and copies ran while one was open for 4% -> 10% of each run, Pallas kernels for 0% -> 0%
where the time goes in v1:
time: 70.6 us; the launch traced here: 70.3 us
  Pallas kernels  42.3 us (60%)
  blocking collectives  7.77 us (11%)
  matrix products  6.95 us (10%)
  local copies, waits for them, and re-layouts  4.68 us (7%)
  other arithmetic  4.61 us (7%)
  starting transfers between devices  2.72 us (4%)
  between operations  1.18 us (2%)
    pallas_call x1, Pallas kernels, sum_everywhere(): pl.pallas_call(functools.partial(sum_kernel, steps, rows), out_shape=(jax...  42.3 us
    psum x1, blocking collectives, body(): lax.psum((flat_values.sum(axis=0), (flat_values * flat_values).sum(axis=0...  4.37 us
    psum x1, blocking collectives, body(): lax.psum((normed_grad.reshape(-1, channels).sum(axis=0), (normed_grad * n...  3.41 us
    dot_general x9, matrix products, kernel_terms(): lax.dot_general(columns, grad_flat, (((0,), (0,)), ((), ())), preferred_e...  2.82 us
    ppermute x2, starting transfers between devices, from_behind(): return lax.ppermute(x, axis, pairs)  2.72 us
    dot_general x9, matrix products, spread_back(): jnp.dot(columns, weight_turned[tap_time, tap_row].reshape(3 * channels, c...  2.36 us
    unnamed x9, local copies, waits for them, and re-layouts  2.06 us
    dot_general x9, matrix products, plane_back(): jnp.dot(columns, weight_plane[tap_row].reshape(3 * channels, channels), p...  1.77 us
  transfers between devices with their start and end apart: 2, of which 0 were waited for; matrix products, arithmetic and copies ran while one was open for 10% of the time, Pallas kernels for 0%

profile of v1, /device:TPU:0, one launch (start us, length us, event | category | flops | bytes accessed | tf_op | source)
XLA Modules:
  0.0 70.3 jit_solution(8597777140334082125)
XLA Ops:
  0.6 1.4 %collective-permute-start = (bf16[2,16,16,128]{3,2,1,0:T(8,128)(2,1)}, bf16[2,16,16,128]{3,2,1,0:T(8,128)(2,1)S(1)}, u32[]{:S(2)}, u32[]{:S(2)}) collective-permute-start(bf16[2,16,16,128]{3,2,1,0:T(8,128)(2,1)} %bitcast.166), channel_id=1, source_target_pairs={{1,0},{3,2},{5,4},{7,6},{9,8},{11,10},{13,12},{15,14},{17,16},{19,... | collective-permute-start | bytes 393224 | tf_op jit(solution)/shard_map/ppermute | solution.py:18
  2.1 2.0 %copy.10 = bf16[3,3,3,128,128]{3,4,2,1,0:T(8,128)(2,1)S(1)} copy(bf16[3,3,3,128,128]{4,3,2,1,0:T(8,128)(2,1)} %param.11) | data formatting | bytes 1769472 | tf_op args[2]
  4.1 0.1 fusion.44
  4.2 0.1 fusion.15
  4.3 0.1 reshape.237
  4.4 0.1 reshape.235
  4.5 4.4 %all-reduce.5 = (f32[32,4]{1,0:T(8,128)S(1)}, f32[32,4]{1,0:T(8,128)S(1)}) all-reduce(f32[32,4]{1,0:T(8,128)S(1)} %reshape.237, f32[32,4]{1,0:T(8,128)S(1)} %reshape.235), channel_id=1, replica_groups=mesh['dp'=16,'ctx'=2] {'ctx'}, use_global_device_ids=true, to_apply=%region_4.0 | all-reduce | flops 256 | bytes 2048 | tf_op jit(solution)/shard_map/psum | solution.py:217
  8.9 0.1 reduce_sum.93
  9.0 0.1 broadcast_in_dim.23
  9.1 0.1 reshape.238
  9.2 0.1 reduce_sum.91
  9.4 0.1 reshape.236
  9.5 0.1 pad.39.clone
  9.6 2.2 %conditional.1 = (f32[1,16,16,128]{3,2,1,0:T(8,128)S(1)}) conditional(s32[]{:T(128)} %convert_element_type.31, () %tuple.20, (bf16[2,16,16,128]{3,2,1,0:T(8,128)(2,1)S(1)}, bf16[3,3,3,128,128]{4,3,2,1,0:T(8,128)(2,1)S(1)}) %tuple.119), branch_computations={%region_6.7_spmd, %region_7.8_spmd} | conditional | flops 230883328 | bytes 9207816 | solution.py:249
  9.7 0.2 pad_slice_fusion.2
  9.9 0.2 fusion.45
  10.1 0.2 convolution_add_fusion.5
  10.4 0.2 convolution_add_fusion.4
  10.6 0.2 fusion.46
  10.8 0.2 convolution_add_fusion.3
  11.1 0.2 convolution_add_fusion.2
  11.3 0.2 fusion.47
  11.5 0.2 convolution_add_fusion.1
  11.7 0.2 fusion.1
  11.9 0.4 pad_slice_fusion.42
  12.3 0.1 pad_slice_fusion.41
  12.5 0.1 pad_maximum_fusion.7
  12.6 0.3 fusion.48
  12.9 0.3 convolution_add_fusion.13
  13.1 0.1 pad_maximum_fusion.9
  13.3 0.3 convolution_add_fusion.12
  13.5 0.3 convolution_add_fusion.11
  13.8 0.1 pad_maximum_fusion.11
  13.9 0.3 convolution_add_fusion.10
  14.2 0.3 convolution_add_fusion.9
  14.5 0.1 pad_maximum_fusion.13
  14.6 0.3 convolution_add_fusion.8
  14.9 0.3 convolution_add_fusion.7
  15.2 0.3 convolution_add_fusion.6
  15.5 0.2 fusion.36
  15.7 1.3 %collective-permute-start.1 = (bf16[2,16,16,128]{3,2,1,0:T(8,128)(2,1)S(1)}, bf16[2,16,16,128]{3,2,1,0:T(8,128)(2,1)S(1)}, u32[]{:S(2)}, u32[]{:S(2)}) collective-permute-start(bf16[2,16,16,128]{3,2,1,0:T(8,128)(2,1)S(1)} %get-tuple-element.132), channel_id=1, source_target_pairs={{0,1},{2,3},{4,5},{6,7},{8,9},{10,11},{12,13},{14,15},{16,17},{18,... | collective-permute-start | bytes 393224 | tf_op jit(solution)/shard_map/ppermute | solution.py:18
  17.0 0.1 reshape.250
  17.1 0.1 reshape.249
  17.2 3.4 %all-reduce.4 = (f32[32,4]{1,0:T(8,128)S(1)}, f32[32,4]{1,0:T(8,128)S(1)}) all-reduce(f32[32,4]{1,0:T(8,128)S(1)} %reshape.250, f32[32,4]{1,0:T(8,128)S(1)} %reshape.249), channel_id=1, replica_groups=mesh['dp'=16,'ctx'=2] {'ctx'}, use_global_device_ids=true, to_apply=%region_12.13 | all-reduce | flops 256 | bytes 2048 | tf_op jit(solution)/shard_map/psum | solution.py:254
  20.7 0.1 reduce_sum.97
  20.8 0.1 broadcast_in_dim.25
  20.9 0.1 mul.100
  21.0 0.1 reduce_sum.95
  21.2 0.1 sub.35
  21.3 0.7 %fusion.37 = bf16[1,2,16,16,128]{4,3,2,1,0:T(8,128)(2,1)} fusion(bf16[1,2,16,16,128]{4,3,2,1,0:T(8,128)(2,1)S(1)} %copy-done.1, f32[2,16,16,128]{3,2,1,0:T(8,128)S(1)} %get-tuple-element.40, f32[128]{0:T(128)S(1)} %mul.100, f32[128]{0:T(128)S(1)} %sub.35, f32[128]{0:T(128)S(1)} %copy-done.2, f32[128]{0:T(128)S(1)} %reshape.238, f32[128]{0:T(128)S(1)} %add_rsqrt_fusion), kind=kLoop, calls=%fused_computation.159 | loop fusion | flops 589824 | bytes 526848 | tf_op jit(solution)/shard_map/broadcast_in_dim | solution.py:263
  22.1 0.4 pad_slice_fusion.18
  22.5 0.1 pad_slice_fusion.17
  22.8 0.3 convolution_dynamic-update-slice_fusion.8
  23.2 0.3 convolution_dynamic-update-slice_fusion.7
  23.5 0.3 convolution_dynamic-update-slice_fusion.6
  23.9 0.3 convolution_dynamic-update-slice_fusion.5
  24.3 0.3 convolution_dynamic-update-slice_fusion.4
  24.7 0.3 convolution_dynamic-update-slice_fusion.3
  25.1 0.3 convolution_dynamic-update-slice_fusion.2
  25.5 0.3 convolution_dynamic-update-slice_fusion.1
  25.8 0.3 convolution_dynamic-update-slice_fusion
  26.2 42.3 %shard_map.84 = (bf16[3584,128]{1,0:T(8,128)(2,1)S(1)}, f32[8,128]{1,0:T(8,128)S(1)}) custom-call(f32[3584,128]{1,0:T(8,128)S(1)} %broadcast_dynamic-update-slice_fusion.kern_ref, f32[8,128]{1,0:T(8,128)S(1)} %maximum_maximum_fusion.small_ref), custom_call_target="tpu_custom_call" | custom-call | tf_op jit(solution)/shard_map/pallas_call | solution.py:186
  68.5 1.3 %convert_multiply_fusion = f32[3456,128]{1,0:T(8,128)} fusion(bf16[3584,128]{1,0:T(8,128)(2,1)S(1)} %get-tuple-element.28), kind=kLoop, calls=%fused_computation.39 | loop fusion | flops 884736 | bytes 2654208 | tf_op jit(solution)/shard_map/mul | solution.py:276
  69.8 0.5 multiply_bitcast_fusion
  (43 shorter events, 1.1 us)
Async XLA Ops:
  0.6 3.6 %copy-start.1 = (bf16[1,2,16,16,128]{4,3,2,1,0:T(8,128)(2,1)S(1)}, bf16[1,2,16,16,128]{4,3,2,1,0:T(8,128)(2,1)}, u32[]{:S(2)}) copy-start(bf16[1,2,16,16,128]{4,3,2,1,0:T(8,128)(2,1)} %param.9) | copy-start | bytes 393220
  0.6 11.3 %collective-permute-start = (bf16[2,16,16,128]{3,2,1,0:T(8,128)(2,1)}, bf16[2,16,16,128]{3,2,1,0:T(8,128)(2,1)S(1)}, u32[]{:S(2)}, u32[]{:S(2)}) collective-permute-start(bf16[2,16,16,128]{3,2,1,0:T(8,128)(2,1)} %bitcast.166), channel_id=1, source_target_pairs={{1,0},{3,2},{5,4},{7,6},{9,8},{11,10},{13,12},{15,14},{17,16},{19,... | collective-permute-start | bytes 393224 | tf_op jit(solution)/shard_map/ppermute | solution.py:18
  2.1 7.5 %copy-start = (bf16[1,2,16,16,128]{4,3,2,1,0:T(8,128)(2,1)S(1)}, bf16[1,2,16,16,128]{4,3,2,1,0:T(8,128)(2,1)}, u32[]{:S(2)}) copy-start(bf16[1,2,16,16,128]{4,3,2,1,0:T(8,128)(2,1)} %param.10) | copy-start | bytes 393220
  14.6 0.9 %copy-start.2 = (f32[128]{0:T(128)S(1)}, f32[128]{0:T(128)}, u32[]{:S(2)}) copy-start(f32[128]{0:T(128)} %param.12) | copy-start | bytes 1540
  14.6 0.9 %copy-start.3 = (f32[128]{0:T(128)S(1)}, f32[128]{0:T(128)}, u32[]{:S(2)}) copy-start(f32[128]{0:T(128)} %param.13) | copy-start | bytes 1540
  15.7 6.4 %collective-permute-start.1 = (bf16[2,16,16,128]{3,2,1,0:T(8,128)(2,1)S(1)}, bf16[2,16,16,128]{3,2,1,0:T(8,128)(2,1)S(1)}, u32[]{:S(2)}, u32[]{:S(2)}) collective-permute-start(bf16[2,16,16,128]{3,2,1,0:T(8,128)(2,1)S(1)} %get-tuple-element.132), channel_id=1, source_target_pairs={{0,1},{2,3},{4,5},{6,7},{8,9},{10,11},{12,13},{14,15},{16,17},{18,... | collective-permute-start | bytes 393224 | tf_op jit(solution)/shard_map/ppermute | solution.py:18

commit v2 on v1

--- a/solution.py
+++ b/solution.py
@@ -88,13 +88,18 @@
     return total_grad.reshape(side_len, side_len, channels)
 
 
-def step_list(dp_count, ctx_count):
+def step_list(dp_count, ctx_count, swapped):
     steps = []
     for axis, count in (("ctx", ctx_count), ("dp", dp_count)):
+        bits = []
         bit = 1
         while bit < count:
-            steps.append((axis, bit))
+            bits.append(bit)
             bit *= 2
+        if swapped and axis == "dp":
+            for i in range(0, len(bits) - 1, 2):
+                bits[i], bits[i + 1] = bits[i + 1], bits[i]
+        steps.extend((axis, bit) for bit in bits)
     return steps
 
 
@@ -102,21 +107,22 @@
     return step in (1, 2)
 
 
-def sum_kernel(steps, rows, kern_ref, small_ref, out_ref, small_out, acc, gath, *rest):
-    count = len(steps)
-    recvs = rest[:count]
-    sends = dict(zip([i for i in range(count) if narrow(i)], rest[count:]))
-    small_send, small_recv, sems_s, sems_r, small_s, small_r, back_s, back_r = rest[-8:]
-    partners = [{axis: lax.axis_index(axis) ^ bit} for axis, bit in steps]
+def sum_kernel(plans, kern_ref, small_ref, out_ref, small_out, acc, gath, *rest):
+    count = len(plans[0][0])
+    rest = list(rest)
+    recvs = [[rest.pop(0) for _ in range(count)] for _ in plans]
+    sends = [{i: rest.pop(0) for i in range(count) if narrow(i)} for _ in plans]
+    small_send, small_recv, sems_s, sems_r, small_s, small_r, back_s, back_r = rest
+    partners = [[{axis: lax.axis_index(axis) ^ bit} for axis, bit in plan[0]] for plan in plans]
     barrier = pltpu.get_barrier_semaphore()
-    for partner in partners:
+    for partner in partners[0]:
         pl.semaphore_signal(
             barrier, inc=1, device_id=partner, device_id_type=pl.DeviceIdType.MESH
         )
     pl.semaphore_wait(barrier, count)
 
     def remote(src, dst, send_sem, recv_sem, partner):
-        return pltpu.make_async_remote_copy(
+        copy = pltpu.make_async_remote_copy(
             src_ref=src,
             dst_ref=dst,
             send_sem=send_sem,
@@ -124,67 +130,97 @@
             device_id=partner,
             device_id_type=pl.DeviceIdType.MESH,
         )
-
-    start = jnp.int32(0)
-    length = rows
-    small_now = small_ref[...]
-    starts = []
-    for i, (axis, bit) in enumerate(steps):
-        starts.append((start, length))
+        copy.start()
+        return copy
+
+    def begin(p, i, start, length):
+        axis, bit = plans[p][0][i]
         half = length // 2
         mine = (lax.axis_index(axis) // bit) % 2
         keep = pl.multiple_of(start + mine * half, 16)
         away = pl.multiple_of(start + (1 - mine) * half, 16)
         held = kern_ref if i == 0 else acc
         if narrow(i):
-            sends[i][...] = held[pl.ds(away, half), :].astype(jnp.bfloat16)
-            source = sends[i]
+            sends[p][i][...] = held[pl.ds(away, half), :].astype(jnp.bfloat16)
+            source = sends[p][i]
         else:
             source = held.at[pl.ds(away, half), :]
-        small_send[i] = small_now
-        copy = remote(source, recvs[i], sems_s.at[i], sems_r.at[i], partners[i])
-        copy.start()
-        small_copy = remote(
-            small_send.at[i], small_recv.at[i], small_s.at[i], small_r.at[i], partners[i]
+        copy = remote(source, recvs[p][i], sems_s.at[p, i], sems_r.at[p, i], partners[p][i])
+        return copy, held, keep, half
+
+    def begin_small(i, value):
+        small_send[i] = value
+        return remote(
+            small_send.at[i], small_recv.at[i], small_s.at[i], small_r.at[i], partners[0][i]
         )
-        small_copy.start()
-        copy.wait()
-        acc[pl.ds(keep, half), :] = held[pl.ds(keep, half), :] + recvs[i][...].astype(jnp.float32)
+
+    spans = [[(plan[1], plan[2])] for plan in plans]
+    flights = [begin(p, 0, plan[1], plan[2]) for p, plan in enumerate(plans)]
+    small_now = small_ref[...]
+    small_copy = begin_small(0, small_now)
+    for i in range(count):
+        for p in range(len(plans)):
+            copy, held, keep, half = flights[p]
+            copy.wait()
+            acc[pl.ds(keep, half), :] = held[pl.ds(keep, half), :] + recvs[p][i][...].astype(
+                jnp.float32
+            )
+            spans[p].append((keep, half))
+            if i + 1 < count:
+                flights[p] = begin(p, i + 1, keep, half)
         small_copy.wait()
         small_now = small_now + small_recv[i]
-        start = keep
-        length = half
+        if i + 1 < count:
+            small_copy = begin_small(i + 1, small_now)
     small_out[...] = small_now
-    gath[pl.ds(start, length), :] = acc[pl.ds(start, length), :].astype(jnp.bfloat16)
+
+    def begin_back(p, i):
+        start, length = spans[p][i + 1]
+        piece = gath.at[pl.ds(start, length), :]
+        return remote(piece, piece, back_s.at[p, i], back_r.at[p, i], partners[p][i])
+
+    for p in range(len(plans)):
+        start, length = spans[p][count]
+        gath[pl.ds(start, length), :] = acc[pl.ds(start, length), :].astype(jnp.bfloat16)
+        flights[p] = begin_back(p, count - 1)
     for i in reversed(range(count)):
-        piece = gath.at[pl.ds(start, length), :]
-        copy = remote(piece, piece, back_s.at[i], back_r.at[i], partners[i])
-        copy.start()
-        copy.wait()
-        start, length = starts[i]
-        start = pl.multiple_of(start, 16)
+        for p in range(len(plans)):
+            flights[p].wait()
+            if i > 0:
+                flights[p] = begin_back(p, i - 1)
     out_ref[...] = gath[...]
 
 
 def sum_everywhere(pieces, small, channels):
-    steps = step_list(lax.axis_size("dp"), lax.axis_size("ctx"))
-    count = len(steps)
-    devices = 2**count
+    dp_count, ctx_count = lax.axis_size("dp"), lax.axis_size("ctx")
+    unit = 16 * dp_count * ctx_count
     used = sum(piece.shape[0] for piece in pieces)
-    unit = 16 * devices
-    rows = -(-used // unit) * unit
-    blank = jnp.zeros((rows - used, channels), jnp.float32)
-    stacked = jnp.concatenate(list(pieces) + [blank], axis=0)
+    units = -(-used // unit)
+    rows = units * unit
+    first = (units + 1) // 2 * unit
+    plans = [(step_list(dp_count, ctx_count, False), 0, first)]
+    if first < rows:
+        plans.append((step_list(dp_count, ctx_count, True), first, rows - first))
+    count = len(plans[0][0])
+    stacked = list(pieces)
+    if rows > used:
+        stacked.append(jnp.zeros((rows - used, channels), jnp.float32))
+    stacked = jnp.concatenate(stacked, axis=0)
     recvs = [
-        pltpu.VMEM((rows >> (i + 1), channels), jnp.bfloat16 if narrow(i) else jnp.float32)
+        pltpu.VMEM((plan[2] >> (i + 1), channels), jnp.bfloat16 if narrow(i) else jnp.float32)
+        for plan in plans
         for i in range(count)
     ]
     sends = [
-        pltpu.VMEM((rows >> (i + 1), channels), jnp.bfloat16) for i in range(count) if narrow(i)
+        pltpu.VMEM((plan[2] >> (i + 1), channels), jnp.bfloat16)
+        for plan in plans
+        for i in range(count)
+        if narrow(i)
     ]
     vmem = pl.BlockSpec(memory_space=pltpu.VMEM)
+    many, one = (len(plans), count), (count,)
     total, small_total = pl.pallas_call(
-        functools.partial(sum_kernel, steps, rows),
+        functools.partial(sum_kernel, plans),
         out_shape=(
             jax.ShapeDtypeStruct((rows, channels), jnp.bfloat16),
             jax.ShapeDtypeStruct(small.shape, jnp.float32),
@@ -198,7 +234,7 @@
             *sends,
             pltpu.VMEM((count,) + small.shape, jnp.float32),
             pltpu.VMEM((count,) + small.shape, jnp.float32),
-            *[pltpu.SemaphoreType.DMA((count,)) for _ in range(6)],
+            *[pltpu.SemaphoreType.DMA(shape) for shape in (many, many, one, one, many, many)],
         ],
         compiler_params=pltpu.CompilerParams(
             collective_id=0, has_side_effects=True, vmem_limit_bytes=48 * 1024 * 1024

time: 70.6 us -> 66.1 us (0.936)
  Pallas kernels: 42.3 us -> 37.9 us
    pallas_call x1, Pallas kernels: 42.3 us -> 37.9 us  [sum_everywhere(): pl.pallas_call(functools.partial(sum_kernel, plans), out_shape=(jax.Shape...]
where the time goes in v2:
time: 66.1 us; the launch traced here: 65.9 us
  Pallas kernels  37.9 us (57%)
  blocking collectives  7.77 us (12%)
  matrix products  6.95 us (11%)
  local copies, waits for them, and re-layouts  4.68 us (7%)
  other arithmetic  4.61 us (7%)
  starting transfers between devices  2.72 us (4%)
  between operations  1.18 us (2%)
    pallas_call x1, Pallas kernels, sum_everywhere(): pl.pallas_call(functools.partial(sum_kernel, plans), out_shape=(jax.Shape...  37.9 us
    psum x1, blocking collectives, body(): lax.psum((flat_values.sum(axis=0), (flat_values * flat_values).sum(axis=0...  4.37 us
    psum x1, blocking collectives, body(): lax.psum((normed_grad.reshape(-1, channels).sum(axis=0), (normed_grad * n...  3.41 us
    dot_general x9, matrix products, kernel_terms(): lax.dot_general(columns, grad_flat, (((0,), (0,)), ((), ())), preferred_e...  2.82 us
    ppermute x2, starting transfers between devices, from_behind(): return lax.ppermute(x, axis, pairs)  2.72 us
    dot_general x9, matrix products, spread_back(): jnp.dot(columns, weight_turned[tap_time, tap_row].reshape(3 * channels, c...  2.36 us
    unnamed x9, local copies, waits for them, and re-layouts  2.06 us
    dot_general x9, matrix products, plane_back(): jnp.dot(columns, weight_plane[tap_row].reshape(3 * channels, channels), p...  1.77 us
  transfers between devices with their start and end apart: 2, of which 0 were waited for; matrix products, arithmetic and copies ran while one was open for 10% of the time, Pallas kernels for 0%

profile of v2, /device:TPU:0, one launch (start us, length us, event | category | flops | bytes accessed | tf_op | source)
XLA Modules:
  0.0 65.9 jit_solution(2567511971728121273)
XLA Ops:
  0.6 1.4 %collective-permute-start = (bf16[2,16,16,128]{3,2,1,0:T(8,128)(2,1)}, bf16[2,16,16,128]{3,2,1,0:T(8,128)(2,1)S(1)}, u32[]{:S(2)}, u32[]{:S(2)}) collective-permute-start(bf16[2,16,16,128]{3,2,1,0:T(8,128)(2,1)} %bitcast.166), channel_id=1, source_target_pairs={{1,0},{3,2},{5,4},{7,6},{9,8},{11,10},{13,12},{15,14},{17,16},{19,... | collective-permute-start | bytes 393224 | tf_op jit(solution)/shard_map/ppermute | solution.py:18
  2.1 2.0 %copy.10 = bf16[3,3,3,128,128]{3,4,2,1,0:T(8,128)(2,1)S(1)} copy(bf16[3,3,3,128,128]{4,3,2,1,0:T(8,128)(2,1)} %param.11) | data formatting | bytes 1769472 | tf_op args[2]
  4.1 0.1 fusion.44
  4.2 0.1 fusion.15
  4.3 0.1 reshape.237
  4.4 0.1 reshape.235
  4.5 4.4 %all-reduce.5 = (f32[32,4]{1,0:T(8,128)S(1)}, f32[32,4]{1,0:T(8,128)S(1)}) all-reduce(f32[32,4]{1,0:T(8,128)S(1)} %reshape.237, f32[32,4]{1,0:T(8,128)S(1)} %reshape.235), channel_id=1, replica_groups=mesh['dp'=16,'ctx'=2] {'ctx'}, use_global_device_ids=true, to_apply=%region_4.0 | all-reduce | flops 256 | bytes 2048 | tf_op jit(solution)/shard_map/psum | solution.py:253
  8.9 0.1 reduce_sum.93
  9.0 0.1 broadcast_in_dim.23
  9.1 0.1 reshape.238
  9.2 0.1 reduce_sum.91
  9.4 0.1 reshape.236
  9.5 0.1 pad.39.clone
  9.6 2.2 %conditional.1 = (f32[1,16,16,128]{3,2,1,0:T(8,128)S(1)}) conditional(s32[]{:T(128)} %convert_element_type.31, () %tuple.20, (bf16[2,16,16,128]{3,2,1,0:T(8,128)(2,1)S(1)}, bf16[3,3,3,128,128]{4,3,2,1,0:T(8,128)(2,1)S(1)}) %tuple.119), branch_computations={%region_6.7_spmd, %region_7.8_spmd} | conditional | flops 230883328 | bytes 9207816 | solution.py:285
  9.7 0.2 pad_slice_fusion.2
  9.9 0.2 fusion.45
  10.1 0.2 convolution_add_fusion.5
  10.4 0.2 convolution_add_fusion.4
  10.6 0.2 fusion.46
  10.8 0.2 convolution_add_fusion.3
  11.1 0.2 convolution_add_fusion.2
  11.3 0.2 fusion.47
  11.5 0.2 convolution_add_fusion.1
  11.7 0.2 fusion.1
  11.9 0.4 pad_slice_fusion.42
  12.3 0.1 pad_slice_fusion.41
  12.5 0.1 pad_maximum_fusion.7
  12.6 0.3 fusion.48
  12.9 0.3 convolution_add_fusion.13
  13.1 0.1 pad_maximum_fusion.9
  13.3 0.3 convolution_add_fusion.12
  13.5 0.3 convolution_add_fusion.11
  13.8 0.1 pad_maximum_fusion.11
  13.9 0.3 convolution_add_fusion.10
  14.2 0.3 convolution_add_fusion.9
  14.5 0.1 pad_maximum_fusion.13
  14.6 0.3 convolution_add_fusion.8
  14.9 0.3 convolution_add_fusion.7
  15.2 0.3 convolution_add_fusion.6
  15.5 0.2 fusion.36
  15.7 1.3 %collective-permute-start.1 = (bf16[2,16,16,128]{3,2,1,0:T(8,128)(2,1)S(1)}, bf16[2,16,16,128]{3,2,1,0:T(8,128)(2,1)S(1)}, u32[]{:S(2)}, u32[]{:S(2)}) collective-permute-start(bf16[2,16,16,128]{3,2,1,0:T(8,128)(2,1)S(1)} %get-tuple-element.132), channel_id=1, source_target_pairs={{0,1},{2,3},{4,5},{6,7},{8,9},{10,11},{12,13},{14,15},{16,17},{18,... | collective-permute-start | bytes 393224 | tf_op jit(solution)/shard_map/ppermute | solution.py:18
  17.0 0.1 reshape.250
  17.1 0.1 reshape.249
  17.2 3.4 %all-reduce.4 = (f32[32,4]{1,0:T(8,128)S(1)}, f32[32,4]{1,0:T(8,128)S(1)}) all-reduce(f32[32,4]{1,0:T(8,128)S(1)} %reshape.250, f32[32,4]{1,0:T(8,128)S(1)} %reshape.249), channel_id=1, replica_groups=mesh['dp'=16,'ctx'=2] {'ctx'}, use_global_device_ids=true, to_apply=%region_12.13 | all-reduce | flops 256 | bytes 2048 | tf_op jit(solution)/shard_map/psum | solution.py:290
  20.7 0.1 reduce_sum.97
  20.8 0.1 broadcast_in_dim.25
  20.9 0.1 mul.100
  21.0 0.1 reduce_sum.95
  21.2 0.1 sub.35
  21.3 0.7 %fusion.37 = bf16[1,2,16,16,128]{4,3,2,1,0:T(8,128)(2,1)} fusion(bf16[1,2,16,16,128]{4,3,2,1,0:T(8,128)(2,1)S(1)} %copy-done.1, f32[2,16,16,128]{3,2,1,0:T(8,128)S(1)} %get-tuple-element.40, f32[128]{0:T(128)S(1)} %mul.100, f32[128]{0:T(128)S(1)} %sub.35, f32[128]{0:T(128)S(1)} %copy-done.2, f32[128]{0:T(128)S(1)} %reshape.238, f32[128]{0:T(128)S(1)} %add_rsqrt_fusion), kind=kLoop, calls=%fused_computation.159 | loop fusion | flops 589824 | bytes 526848 | tf_op jit(solution)/shard_map/broadcast_in_dim | solution.py:299
  22.1 0.4 pad_slice_fusion.18
  22.5 0.1 pad_slice_fusion.17
  22.8 0.3 convolution_dynamic-update-slice_fusion.8
  23.2 0.3 convolution_dynamic-update-slice_fusion.7
  23.5 0.3 convolution_dynamic-update-slice_fusion.6
  23.9 0.3 convolution_dynamic-update-slice_fusion.5
  24.3 0.3 convolution_dynamic-update-slice_fusion.4
  24.7 0.3 convolution_dynamic-update-slice_fusion.3
  25.1 0.3 convolution_dynamic-update-slice_fusion.2
  25.5 0.3 convolution_dynamic-update-slice_fusion.1
  25.8 0.3 convolution_dynamic-update-slice_fusion
  26.2 37.9 %shard_map.84 = (bf16[3584,128]{1,0:T(8,128)(2,1)S(1)}, f32[8,128]{1,0:T(8,128)S(1)}) custom-call(f32[3584,128]{1,0:T(8,128)S(1)} %broadcast_dynamic-update-slice_fusion.kern_ref, f32[8,128]{1,0:T(8,128)S(1)} %maximum_maximum_fusion.small_ref), custom_call_target="tpu_custom_call" | custom-call | tf_op jit(solution)/shard_map/pallas_call | solution.py:222
  64.1 1.3 %convert_multiply_fusion = f32[3456,128]{1,0:T(8,128)} fusion(bf16[3584,128]{1,0:T(8,128)(2,1)S(1)} %get-tuple-element.28), kind=kLoop, calls=%fused_computation.39 | loop fusion | flops 884736 | bytes 2654208 | tf_op jit(solution)/shard_map/mul | solution.py:312
  65.4 0.5 multiply_bitcast_fusion
  (43 shorter events, 1.1 us)
Async XLA Ops:
  0.6 3.6 %copy-start.1 = (bf16[1,2,16,16,128]{4,3,2,1,0:T(8,128)(2,1)S(1)}, bf16[1,2,16,16,128]{4,3,2,1,0:T(8,128)(2,1)}, u32[]{:S(2)}) copy-start(bf16[1,2,16,16,128]{4,3,2,1,0:T(8,128)(2,1)} %param.9) | copy-start | bytes 393220
  0.6 11.3 %collective-permute-start = (bf16[2,16,16,128]{3,2,1,0:T(8,128)(2,1)}, bf16[2,16,16,128]{3,2,1,0:T(8,128)(2,1)S(1)}, u32[]{:S(2)}, u32[]{:S(2)}) collective-permute-start(bf16[2,16,16,128]{3,2,1,0:T(8,128)(2,1)} %bitcast.166), channel_id=1, source_target_pairs={{1,0},{3,2},{5,4},{7,6},{9,8},{11,10},{13,12},{15,14},{17,16},{19,... | collective-permute-start | bytes 393224 | tf_op jit(solution)/shard_map/ppermute | solution.py:18
  2.1 7.5 %copy-start = (bf16[1,2,16,16,128]{4,3,2,1,0:T(8,128)(2,1)S(1)}, bf16[1,2,16,16,128]{4,3,2,1,0:T(8,128)(2,1)}, u32[]{:S(2)}) copy-start(bf16[1,2,16,16,128]{4,3,2,1,0:T(8,128)(2,1)} %param.10) | copy-start | bytes 393220
  14.6 0.9 %copy-start.2 = (f32[128]{0:T(128)S(1)}, f32[128]{0:T(128)}, u32[]{:S(2)}) copy-start(f32[128]{0:T(128)} %param.12) | copy-start | bytes 1540
  14.6 0.9 %copy-start.3 = (f32[128]{0:T(128)S(1)}, f32[128]{0:T(128)}, u32[]{:S(2)}) copy-start(f32[128]{0:T(128)} %param.13) | copy-start | bytes 1540
  15.7 6.4 %collective-permute-start.1 = (bf16[2,16,16,128]{3,2,1,0:T(8,128)(2,1)S(1)}, bf16[2,16,16,128]{3,2,1,0:T(8,128)(2,1)S(1)}, u32[]{:S(2)}, u32[]{:S(2)}) collective-permute-start(bf16[2,16,16,128]{3,2,1,0:T(8,128)(2,1)S(1)} %get-tuple-element.132), channel_id=1, source_target_pairs={{0,1},{2,3},{4,5},{6,7},{8,9},{10,11},{12,13},{14,15},{16,17},{18,... | collective-permute-start | bytes 393224 | tf_op jit(solution)/shard_map/ppermute | solution.py:18
